TPU v7x, 128 devices: a whole 4x4x4 slice. The times are simulated.
128 devices in a mesh: row: 8 (over z_lo, x), col: 16 (over y, z_hi, core).
Axes of the slice: x: 4, y: 4, z: 4 (z_hi: 2, z_lo: 2; z = z_hi * 2 + z_lo), core: 2. Of those that a mesh axis runs over, the one named last changes fastest.
Arguments:
- theta_one: bfloat16 [8192, 4096], P('row', 'col'), may hold values from -4 to 4
- theta_two: bfloat16 [4096, 32768], P('row', 'col'), may hold values from -4 to 4
- cost_one: bfloat16 [8192, 4096], P('row', 'col'), may hold values from -3 to 3
- cost_two: bfloat16 [4096, 32768], P('row', 'col'), may hold values from -3 to 3
- depot_price: float32 [8192], P('row'), may hold values from 0.5 to 2
- hub_price: float32 [4096], replicated, may hold values from -3 to 3
- zone_price: float32 [32768], P('col'), may hold values from 0.5 to 2
- mask_one: int32 [64, 32], P('row', 'col'), may hold values 0 or 1
- mask_two: int32 [32, 256], P('row', 'col'), may hold values 0 or 1
- supply: int32 [8192], P('row'), may hold values from 1 to 4
- demand: int32 [32768], P('col'), may hold values from 1 to 4
- capacity: int32 [4096], replicated, may hold values from 1 to 8
- cot_flow_one: bfloat16 [8192, 4096], P('row', 'col'), may hold values from -6 to 6
- cot_flow_two: bfloat16 [4096, 32768], P('row', 'col'), may hold values from -6 to 6
- cot_depot: float32 [8192], P('row'), may hold values from -6 to 6
- cot_hub: float32 [4096], replicated, may hold values from -6 to 6
- cot_zone: float32 [32768], P('col'), may hold values from -6 to 6
Outputs:
- grad_theta_one: float32 [8192, 4096], P('row', 'col')
- grad_theta_two: float32 [4096, 32768], P('row', 'col')
- grad_cost_one: float32 [8192, 4096], P('row', 'col')
- grad_cost_two: float32 [4096, 32768], P('row', 'col')
- grad_depot: float32 [8192], P('row')
- grad_hub: float32 [4096], replicated
- grad_zone: float32 [32768], P('col')
All inputs are finite; a program needn't handle non-finite values. No bound on the sum of `mask_one` or of `mask_two` on one device may be relied on, other than what follows from the above.
Results may differ from a plain program's by a relative error of at most 0.0003.
Values sent between devices are 32-bit elements; how exact they have to be, the bound alone decides.
A program may use at most 64 MiB of HBM per device.

v0:
```python
import jax
import jax.numpy as jnp
from jax import lax
from jax.sharding import PartitionSpec as P

DEP = 8192
HUB = 4096
TILE = 128
ITERS = 2


STEP_PRIMAL = 0.5
STEP_DUAL = 0.5
HUB_RATE = 4.0


def expand(tiles, tile_size):
    block_rows, block_cols = tiles.shape
    spread = jnp.broadcast_to(
        tiles.astype(jnp.float32)[:, None, :, None], (block_rows, tile_size, block_cols, tile_size)
    )
    return spread.reshape(block_rows * tile_size, block_cols * tile_size)


def logistic(values):
    return 1.0 / (1.0 + jnp.exp(-values))


def slope(values):
    sigma = logistic(values)
    return sigma * (1.0 - sigma)


def dual_sums(depot_part, hub_one_part, hub_two_part, zone_part):
    depot_sum, hub_two_sum = lax.psum((depot_part, hub_two_part), "col")
    hub_one_sum, zone_sum = lax.psum((hub_one_part, zone_part), "row")
    hub_sum = lax.all_gather(hub_one_sum, "col", axis=0, tiled=True) + lax.all_gather(
        hub_two_sum, "row", axis=0, tiled=True
    )
    return (depot_sum, hub_sum, zone_sum)


def on_device(
    theta_one,
    theta_two,
    cost_one,
    cost_two,
    depot_price,
    hub_price,
    zone_price,
    mask_one,
    mask_two,
    supply,
    demand,
    capacity,
    cot_flow_one,
    cot_flow_two,
    cot_depot,
    cot_hub,
    cot_zone,
):
    hub_cols = theta_one.shape[1]
    hub_rows = theta_two.shape[0]
    start_one = lax.axis_index("col") * hub_cols
    start_two = lax.axis_index("row") * hub_rows
    levels = capacity.astype(jnp.float32)
    level_one = lax.dynamic_slice_in_dim(levels, start_one, hub_cols, 0)
    level_two = lax.dynamic_slice_in_dim(levels, start_two, hub_rows, 0)
    keep_one = expand(mask_one, TILE) * level_one[None, :]
    keep_two = expand(mask_two, TILE) * (0.25 * level_two)[:, None]
    supply_level = 0.5 * supply.astype(jnp.float32)
    demand_level = 0.125 * demand.astype(jnp.float32)
    cost_first = cost_one.astype(jnp.float32)
    cost_second = cost_two.astype(jnp.float32)
    states_one = [theta_one.astype(jnp.float32)]
    states_two = [theta_two.astype(jnp.float32)]
    sigma_one = logistic(states_one[0])
    sigma_two = logistic(states_two[0])
    depot_now, hub_now, zone_now = (depot_price, hub_price, zone_price)
    depot_saved, zone_saved, depot_grow, zone_grow = ([], [], [], [])
    for counter in range(ITERS):
        hub_first = lax.dynamic_slice_in_dim(hub_now, start_one, hub_cols, 0)
        hub_second = lax.dynamic_slice_in_dim(hub_now, start_two, hub_rows, 0)
        next_one = states_one[-1] - STEP_PRIMAL * (
            cost_first + depot_now[:, None] + hub_first[None, :]
        )
        next_two = states_two[-1] - STEP_PRIMAL * (
            cost_second - hub_second[:, None] - zone_now[None, :]
        )
        fresh_one = logistic(next_one)
        fresh_two = logistic(next_two)
        bar_one = keep_one * (2.0 * fresh_one - sigma_one)
        bar_two = keep_two * (2.0 * fresh_two - sigma_two)
        depot_sum, hub_sum, zone_sum = dual_sums(
            jnp.sum(bar_one, axis=1),
            jnp.sum(bar_one, axis=0),
            -jnp.sum(bar_two, axis=1),
            jnp.sum(bar_two, axis=0),
        )
        growth_depot = jnp.exp(STEP_DUAL * (depot_sum / HUB - supply_level))
        growth_zone = jnp.exp(STEP_DUAL * (demand_level - zone_sum / HUB))
        depot_now = depot_now * growth_depot
        zone_now = zone_now * growth_zone
        hub_now = hub_now + HUB_RATE * hub_sum / DEP
        depot_saved.append(depot_now)
        zone_saved.append(zone_now)
        depot_grow.append(growth_depot)
        zone_grow.append(growth_zone)
        states_one.append(next_one)
        states_two.append(next_two)
        sigma_one = fresh_one
        sigma_two = fresh_two
    adj_one = cot_flow_one.astype(jnp.float32) * keep_one * slope(states_one[-1])
    adj_two = cot_flow_two.astype(jnp.float32) * keep_two * slope(states_two[-1])
    adj_depot, adj_hub, adj_zone = (cot_depot, cot_hub, cot_zone)
    grad_first = jnp.zeros_like(adj_one)
    grad_second = jnp.zeros_like(adj_two)
    for counter in range(ITERS - 1, -1, -1):
        push_depot = adj_depot * depot_saved[counter] * (STEP_DUAL / HUB)
        push_zone = -adj_zone * zone_saved[counter] * (STEP_DUAL / HUB)
        push_hub = adj_hub * (HUB_RATE / DEP)
        push_first = lax.dynamic_slice_in_dim(push_hub, start_one, hub_cols, 0)
        push_second = lax.dynamic_slice_in_dim(push_hub, start_two, hub_rows, 0)
        weight_one = push_depot[:, None] + push_first[None, :]
        weight_two = push_zone[None, :] - push_second[:, None]
        total_one = adj_one + 2.0 * weight_one * keep_one * slope(states_one[counter + 1])
        total_two = adj_two + 2.0 * weight_two * keep_two * slope(states_two[counter + 1])
        adj_one = total_one - weight_one * keep_one * slope(states_one[counter])
        adj_two = total_two - weight_two * keep_two * slope(states_two[counter])
        grad_first = grad_first - STEP_PRIMAL * total_one
        grad_second = grad_second - STEP_PRIMAL * total_two
        depot_sum, hub_sum, zone_sum = dual_sums(
            jnp.sum(total_one, axis=1),
            -jnp.sum(total_one, axis=0),
            jnp.sum(total_two, axis=1),
            jnp.sum(total_two, axis=0),
        )
        adj_depot = adj_depot * depot_grow[counter] - STEP_PRIMAL * depot_sum
        adj_hub = adj_hub + STEP_PRIMAL * hub_sum
        adj_zone = adj_zone * zone_grow[counter] + STEP_PRIMAL * zone_sum
    return (adj_one, adj_two, grad_first, grad_second, adj_depot, adj_hub, adj_zone)


def solution(mesh):
    return jax.shard_map(
        on_device,
        mesh=mesh,
        in_specs=(
            P("row", "col"),
            P("row", "col"),
            P("row", "col"),
            P("row", "col"),
            P("row"),
            P(),
            P("col"),
            P("row", "col"),
            P("row", "col"),
            P("row"),
            P("col"),
            P(),
            P("row", "col"),
            P("row", "col"),
            P("row"),
            P(),
            P("col"),
        ),
        out_specs=(
            P("row", "col"),
            P("row", "col"),
            P("row", "col"),
            P("row", "col"),
            P("row"),
            P(),
            P("col"),
        ),
        check_vma=False,
    )
```

profile of v0, /device:TPU:1, one launch (start us, length us, event | category | flops | bytes accessed | tf_op | source)
XLA Modules:
  0.0 391.3 jit_solution(2100825272906211371)
XLA Ops:
  6.0 2.1 fusion.51
  8.5 3.7 fusion.48
  12.3 17.6 %all-reduce.5 = (f32[256]{0:T(256)S(1)}, f32[2048]{0:T(1024)S(1)}) all-reduce(f32[256]{0:T(256)S(1)} %get-tuple-element.17, f32[2048]{0:T(1024)S(1)} %get-tuple-element.11), channel_id=1, replica_groups=mesh['row'=8,'col'=16] {'row'}, use_global_device_ids=true, to_apply=%region_3.0 | all-reduce | flops 2304 | bytes 18432 | tf_op jit(solution)/shard_map/psum | solution.py:36
  29.9 38.2 %all-reduce.2 = (f32[1024]{0:T(1024)S(1)}, f32[512]{0:T(512)S(1)}) all-reduce(f32[1024]{0:T(1024)S(1)} %get-tuple-element.18, f32[512]{0:T(512)S(1)} %neg.47), channel_id=1, replica_groups=mesh['row'=8,'col'=16] {'col'}, use_global_device_ids=true, to_apply=%region_1.0 | all-reduce | flops 1536 | bytes 12288 | tf_op jit(solution)/shard_map/psum | solution.py:35
  68.2 19.1 %all-gather.1 = f32[8,1,512]{2,1,0:T(1,128)S(1)} all-gather(f32[1,1,512]{2,1,0:T(1,128)S(1)} %bitcast.63), channel_id=1, replica_groups=mesh['row'=8,'col'=16] {'row'}, dimensions={0}, use_global_device_ids=true | all-gather | bytes 18432 | tf_op jit(solution)/shard_map/all_gather | solution.py:37
  87.2 25.0 %all-gather = f32[16,1,256]{2,1,0:T(1,128)S(1)} all-gather(f32[1,1,256]{2,1,0:T(1,128)S(1)} %bitcast.66), channel_id=1, replica_groups=mesh['row'=8,'col'=16] {'col'}, dimensions={0}, use_global_device_ids=true | all-gather | bytes 17408 | tf_op jit(solution)/shard_map/all_gather | solution.py:37
  112.4 2.1 multiply_reduce_fusion.1
  114.5 32.7 %psum.101 = f32[1024]{0:T(1024)S(1)} all-reduce(f32[1024]{0:T(1024)S(1)} %multiply_reduce_fusion.1), channel_id=1, replica_groups=mesh['row'=8,'col'=16] {'col'}, use_global_device_ids=true, to_apply=%region_7.0 | all-reduce | flops 1024 | bytes 8192 | tf_op jit(solution)/shard_map/psum | solution.py:35
  147.3 5.9 %multiply_reduce_fusion = f32[2048]{0:T(1024)S(1)} fusion(f32[64,8,16,128]{3,2,1,0:T(8,128)} %bitcast.45, f32[512]{0:T(512)S(1)} %dynamic-slice_multiply_fusion, f32[2048]{0:T(1024)S(1)} %fusion.44, f32[512]{0:T(512)S(1)} %dynamic_slice.36, f32[2048]{0:T(1024)S(1)} %copy-done.8, f32[512]{0:T(512)S(1)} %dynamic_slice.33, bf16[512,2048]{1,0:T(8,128)(2,1)} %param.20, ...), kind=kLoop, calls=%fused_computation.35 | loop fusion | flops 22018048 | bytes 8419328 | tf_op jit(solution)/shard_map/reduce_sum | solution.py:98
  153.2 12.7 %psum.105 = f32[2048]{0:T(1024)S(1)} all-reduce(f32[2048]{0:T(1024)S(1)} %multiply_reduce_fusion), channel_id=1, replica_groups=mesh['row'=8,'col'=16] {'row'}, use_global_device_ids=true, to_apply=%region_15.0 | all-reduce | flops 2048 | bytes 16384 | tf_op jit(solution)/shard_map/psum | solution.py:36
  166.0 3.2 fusion.50
  169.2 8.3 %fusion.47 = (f32[2048]{0:T(1024)S(1)}, f32[512]{0:T(512)S(1)}, f32[512,2048]{1,0:T(8,128)}) fusion(f32[2048]{0:T(1024)S(1)} %fusion.44, f32[512]{0:T(512)S(1)} %dynamic_slice.36, f32[2048]{0:T(1024)S(1)} %copy-done.8, f32[512]{0:T(512)S(1)} %dynamic_slice.33, bf16[512,2048]{1,0:T(8,128)(2,1)S(1)} %copy-done.5, bf16[512,2048]{1,0:T(8,128)(2,1)S(1)} %copy-done.2, ...), kind=kLoop, calls=%fused_computation.99 | loop fusion | flops 25163264 | bytes 14723072 | tf_op jit(solution)/shard_map/reduce_sum | solution.py:136
  177.5 14.7 %all-reduce.4 = (f32[256]{0:T(256)S(1)}, f32[2048]{0:T(1024)S(1)}) all-reduce(f32[256]{0:T(256)S(1)} %neg.49, f32[2048]{0:T(1024)S(1)} %get-tuple-element.9), channel_id=1, replica_groups=mesh['row'=8,'col'=16] {'row'}, use_global_device_ids=true, to_apply=%region_11.0 | all-reduce | flops 2304 | bytes 18432 | tf_op jit(solution)/shard_map/psum | solution.py:36
  192.3 44.3 %all-reduce.1 = (f32[512]{0:T(512)S(1)}, f32[1024]{0:T(1024)S(1)}) all-reduce(f32[512]{0:T(512)S(1)} %get-tuple-element.10, f32[1024]{0:T(1024)S(1)} %get-tuple-element.15), channel_id=1, replica_groups=mesh['row'=8,'col'=16] {'col'}, use_global_device_ids=true, to_apply=%region_17.0 | all-reduce | flops 1536 | bytes 12288 | tf_op jit(solution)/shard_map/psum | solution.py:35
  236.6 19.2 %all-gather.3 = f32[8,1,512]{2,1,0:T(1,128)S(1)} all-gather(f32[1,1,512]{2,1,0:T(1,128)S(1)} %bitcast.64), channel_id=1, replica_groups=mesh['row'=8,'col'=16] {'row'}, dimensions={0}, use_global_device_ids=true | all-gather | bytes 18432 | tf_op jit(solution)/shard_map/all_gather | solution.py:37
  255.8 24.2 %all-gather.2 = f32[16,1,256]{2,1,0:T(1,128)S(1)} all-gather(f32[1,1,256]{2,1,0:T(1,128)S(1)} %bitcast.67), channel_id=1, replica_groups=mesh['row'=8,'col'=16] {'col'}, dimensions={0}, use_global_device_ids=true | all-gather | bytes 17408 | tf_op jit(solution)/shard_map/all_gather | solution.py:37
  280.2 2.7 fusion.49
  282.9 1.9 multiply_subtract_fusion.1
  284.8 5.7 %fusion.46 = (f32[2048]{0:T(1024)S(1)}, f32[512]{0:T(512)S(1)}, f32[512,2048]{1,0:T(8,128)S(1)}) fusion(f32[512]{0:T(512)S(1)} %dynamic_slice.39, f32[2048]{0:T(1024)S(1)} %multiply_multiply_fusion, f32[512,2048]{1,0:T(8,128)S(1)} %copy-done.3, f32[2048]{0:T(1024)S(1)} %copy-done.8, f32[512]{0:T(512)S(1)} %dynamic_slice.33, bf16[512,2048]{1,0:T(8,128)(2,1)} %param.20, ...), kind=kLoop, calls=%fused_computation.98 | loop fusion | flops 24114688 | bytes 16820224 | tf_op jit(solution)/shard_map/reduce_sum | solution.py:136
  290.5 6.2 %multiply_subtract_fusion = (f32[512,2048]{1,0:T(8,128)}, f32[512,2048]{1,0:T(8,128)}) fusion(f32[512,2048]{1,0:T(8,128)S(1)} %get-tuple-element.31, f32[512,2048]{1,0:T(8,128)S(1)} %copy-done.3, bf16[512,2048]{1,0:T(8,128)(2,1)S(1)} %copy-done.2, f32[512]{0:T(512)S(1)} %dynamic-slice_multiply_fusion, f32[64,8,16,128]{3,2,1,0:T(8,128)S(1)} %bitcast.48, ...), kind=kLoop, calls=%fused_computation.34 | loop fusion | flops 15728640 | bytes 23080960 | tf_op jit(solution)/shard_map/sub | solution.py:131
  296.8 12.9 %all-reduce.3 = (f32[256]{0:T(256)S(1)}, f32[2048]{0:T(1024)S(1)}) all-reduce(f32[256]{0:T(256)S(1)} %neg.53, f32[2048]{0:T(1024)S(1)} %get-tuple-element.7), channel_id=1, replica_groups=mesh['row'=8,'col'=16] {'row'}, use_global_device_ids=true, to_apply=%region_23.0 | all-reduce | flops 2304 | bytes 18432 | tf_op jit(solution)/shard_map/psum | solution.py:36
  310.3 36.7 %all-reduce = (f32[1024]{0:T(1024)S(1)}, f32[512]{0:T(512)S(1)}) all-reduce(f32[1024]{0:T(1024)S(1)} %get-tuple-element.14, f32[512]{0:T(512)S(1)} %get-tuple-element.8), channel_id=1, replica_groups=mesh['row'=8,'col'=16] {'col'}, use_global_device_ids=true, to_apply=%region_21.0 | all-reduce | flops 1536 | bytes 12288 | tf_op jit(solution)/shard_map/psum | solution.py:35
  347.6 19.0 %all-gather.5 = f32[8,1,512]{2,1,0:T(1,128)S(1)} all-gather(f32[1,1,512]{2,1,0:T(1,128)S(1)} %bitcast.62), channel_id=1, replica_groups=mesh['row'=8,'col'=16] {'row'}, dimensions={0}, use_global_device_ids=true | all-gather | bytes 18432 | tf_op jit(solution)/shard_map/all_gather | solution.py:37
  366.7 24.0 %all-gather.4 = f32[16,1,256]{2,1,0:T(1,128)S(1)} all-gather(f32[1,1,256]{2,1,0:T(1,128)S(1)} %bitcast.65), channel_id=1, replica_groups=mesh['row'=8,'col'=16] {'col'}, dimensions={0}, use_global_device_ids=true | all-gather | bytes 17408 | tf_op jit(solution)/shard_map/all_gather | solution.py:37
  (63 shorter events, 8.0 us)
Async XLA Ops:
  0.6 7.8 %copy-start.8 = (f32[2048]{0:T(1024)S(1)}, f32[2048]{0:T(1024)}, u32[]{:S(2)}) copy-start(f32[2048]{0:T(1024)} %param.23) | copy-start | bytes 24580
  0.6 7.8 %copy-start.2 = (bf16[512,2048]{1,0:T(8,128)(2,1)S(1)}, bf16[512,2048]{1,0:T(8,128)(2,1)}, u32[]{:S(2)}) copy-start(bf16[512,2048]{1,0:T(8,128)(2,1)} %param.18) | copy-start | bytes 6291460
  3.8 4.7 %copy-start.4 = (bf16[512,2048]{1,0:T(8,128)(2,1)S(1)}, bf16[512,2048]{1,0:T(8,128)(2,1)}, u32[]{:S(2)}) copy-start(bf16[512,2048]{1,0:T(8,128)(2,1)} %param.20) | copy-start | bytes 6291460
  8.4 3.8 copy-start
  8.5 59.6 %copy-start.11 = (f32[1024]{0:T(1024)S(1)}, f32[1024]{0:T(1024)}, u32[]{:S(2)}) copy-start(f32[1024]{0:T(1024)} %param.21) | copy-start | bytes 12292
  8.5 59.6 %copy-start.13 = (s32[1024]{0:T(1024)S(1)}, s32[1024]{0:T(1024)}, u32[]{:S(2)}) copy-start(s32[1024]{0:T(1024)} %param.26) | copy-start | bytes 12292
  8.5 59.7 %copy-start.10 = (s32[2048]{0:T(1024)S(1)}, s32[2048]{0:T(1024)}, u32[]{:S(2)}) copy-start(s32[2048]{0:T(1024)} %param.27) | copy-start | bytes 24580
  8.5 103.7 %copy-start.15 = (f32[4096]{0:T(1024)S(1)}, f32[4096]{0:T(1024)}, u32[]{:S(2)}) copy-start(f32[4096]{0:T(1024)} %param.22) | copy-start | bytes 49156
  8.5 138.7 %copy-start.14 = (f32[1024]{0:T(1024)S(1)}, f32[1024]{0:T(1024)}, u32[]{:S(2)}) copy-start(f32[1024]{0:T(1024)} %param.31) | copy-start | bytes 12292
  147.3 18.7 %copy-start.12 = (f32[2048]{0:T(1024)S(1)}, f32[2048]{0:T(1024)}, u32[]{:S(2)}) copy-start(f32[2048]{0:T(1024)} %param.33) | copy-start | bytes 24580
  165.9 3.3 copy-start.5
  169.2 110.8 %copy-start.9 = (f32[4096]{0:T(1024)S(1)}, f32[4096]{0:T(1024)}, u32[]{:S(2)}) copy-start(f32[4096]{0:T(1024)} %param.32) | copy-start | bytes 49156
  236.5 46.4 %copy-start.6 = (bf16[1024,256]{1,0:T(8,128)(2,1)S(1)}, bf16[1024,256]{1,0:T(8,128)(2,1)}, u32[]{:S(2)}) copy-start(bf16[1024,256]{1,0:T(8,128)(2,1)} %param.17) | copy-start | bytes 1572868
  236.6 46.4 %copy-start.7 = (f32[1024,256]{1,0:T(8,128)S(1)}, f32[1024,256]{1,0:T(8,128)}, u32[]{:S(2)}) copy-start(f32[1024,256]{1,0:T(8,128)} %get-tuple-element.34) | copy-start | bytes 3145732
  280.2 4.7 %copy-start.1 = (f32[4,128,16,128]{3,2,1,0:T(8,128)S(1)}, f32[4,128,16,128]{3,2,1,0:T(8,128)}, u32[]{:S(2)}) copy-start(f32[4,128,16,128]{3,2,1,0:T(8,128)} %copy-done) | copy-start | bytes 12582916
  280.2 4.7 %copy-start.3 = (f32[512,2048]{1,0:T(8,128)S(1)}, f32[512,2048]{1,0:T(8,128)}, u32[]{:S(2)}) copy-start(f32[512,2048]{1,0:T(8,128)} %get-tuple-element.33) | copy-start | bytes 12582916
where the time goes:
time: 392 us; the launch traced here: 391 us
  blocking collectives  340 us (87%)
  other arithmetic  46.9 us (12%)
    psum x4, blocking collectives, dual_sums(): depot_sum, hub_two_sum = lax.psum((depot_part, hub_two_part), 'col')  152 us
    all_gather x3, blocking collectives, dual_sums(): lax.all_gather(hub_one_sum, 'col', axis=0, tiled=True)  73.2 us
    psum x4, blocking collectives, dual_sums(): hub_one_sum, zone_sum = lax.psum((hub_one_part, zone_part), 'row')  58 us
    all_gather x3, blocking collectives, dual_sums(): lax.all_gather(hub_two_sum, 'row', axis=0, tiled=True)  57.3 us
    reduce_sum x2, other arithmetic, on_device(): jnp.sum(total_two, axis=0)  14 us
    reduce_sum x2, other arithmetic, on_device(): jnp.sum(bar_two, axis=0)  9.64 us

commit v1 on v0

v1 whole, which is shorter than its diff:
```python
import functools

import jax
import jax.numpy as jnp
from jax import lax
from jax.experimental import pallas as pl
from jax.experimental.pallas import tpu as pltpu
from jax.sharding import PartitionSpec as P

DEP = 8192
HUB = 4096
TILE = 128
LANES = 128
STEP = 0.5
HUB_RATE = 4.0
CHUNK = 64
MESH = pl.DeviceIdType.MESH
F32 = jnp.float32


def fold(values):
    return jnp.sum(values.reshape(values.shape[0] // 8, 8, LANES), axis=0)


def spread(row):
    return jnp.transpose(jnp.broadcast_to(row, (LANES, LANES)))


def kernel(
    n_row,
    n_col,
    theta_one,
    theta_two,
    cost_one,
    cost_two,
    depot_hbm,
    hub_hbm,
    zone_hbm,
    mask_one,
    mask_two,
    supply_hbm,
    demand_hbm,
    capacity_hbm,
    cot_one,
    cot_two,
    cot_depot_hbm,
    cot_hub_hbm,
    cot_zone_hbm,
    grad_one,
    grad_two,
    grad_cost_one,
    grad_cost_two,
    grad_depot,
    grad_hub,
    grad_zone,
    th1,
    th2,
    co1,
    co2,
    ct1,
    ct2,
    depot,
    hub,
    zone,
    supply,
    demand,
    capacity,
    cot_depot,
    cot_hub,
    cot_zone,
    a1,
    a2,
    b1,
    b2,
    side_depot,
    side_hub,
    side_cap,
    stage_depot,
    stage_hub,
    stage_zone,
    send_d,
    send_z,
    send_h1,
    send_h2,
    got_d,
    got_z,
    got_h1,
    got_h2,
    got_g,
    load_sem,
    small_sem,
    d_out,
    d_in,
    z_out,
    z_in,
    h1_out,
    h1_in,
    h2_out,
    h2_in,
    g_out,
    g_in,
):
    r = lax.axis_index("row")
    c = lax.axis_index("col")
    other = c // 2
    n_d = depot.shape[0]
    n_z = zone.shape[0]
    n_h1 = send_h1.shape[1]
    n_h2 = side_hub.shape[0] // LANES

    bigs = [
        pltpu.make_async_copy(src, dst, load_sem.at[n])
        for n, (src, dst) in enumerate(
            (
                (theta_one, th1),
                (cost_one, co1),
                (theta_two, th2),
                (cost_two, co2),
                (cot_one, ct1),
                (cot_two, ct2),
            )
        )
    ]
    smalls = [
        pltpu.make_async_copy(src, dst, small_sem.at[n])
        for n, (src, dst) in enumerate(
            (
                (depot_hbm, depot),
                (hub_hbm, hub),
                (zone_hbm, zone),
                (capacity_hbm, capacity),
                (supply_hbm, supply),
                (demand_hbm, demand),
                (cot_depot_hbm, cot_depot),
                (cot_hub_hbm, cot_hub),
                (cot_zone_hbm, cot_zone),
            )
        )
    ]
    for copy in smalls + bigs:
        copy.start()

    barrier = pltpu.get_barrier_semaphore()

    def signal(rr, cc):
        pl.semaphore_signal(barrier, inc=1, device_id=(rr, cc), device_id_type=MESH)

    def loop(count, body):
        def step(k, carry):
            body(k)
            return carry

        lax.fori_loop(0, count, step, 0)

    @pl.when(r != other)
    def _():
        loop(n_col, lambda k: signal(other, lax.rem(c + k, n_col)))
        for q in range(2):
            loop(n_row, lambda k: signal(lax.rem(r + k, n_row), 2 * r + q))

    @pl.when(r == other)
    def _():
        loop(n_col - 1, lambda k: signal(r, lax.rem(c + k + 1, n_col)))
        loop(n_row - 1, lambda k: signal(lax.rem(r + k + 1, n_row), c))
        loop(n_row, lambda k: signal(lax.rem(r + k, n_row), c + 1 - 2 * lax.rem(c, 2)))

    loop(n_col - 1, lambda k: signal(r, lax.rem(c + k + 1, n_col)))
    loop(n_row - 1, lambda k: signal(lax.rem(r + k + 1, n_row), c))

    for copy in smalls:
        copy.wait()

    def hub_one(ref, j):
        return ref[pl.ds(c * n_h1 + j, 1), :]

    def hub_two(ref, i):
        return ref[pl.ds(r * n_h2 + i, 1), :]

    level_one = [hub_one(capacity, j).astype(F32) for j in range(n_h1)]
    for i in range(n_h2):
        side_cap[pl.ds(i * LANES, LANES), :] = spread(0.25 * hub_two(capacity, i).astype(F32))

    def set_sides(depot_rows, hub_rows):
        for i in range(n_d):
            side_depot[pl.ds(i * LANES, LANES), :] = spread(depot_rows[i])
        for i in range(n_h2):
            side_hub[pl.ds(i * LANES, LANES), :] = spread(hub_rows[i])

    def sweep_one(body, lanes, rows_out, cols_out):
        def block(i, cols):
            cols = list(cols)
            for s in range(LANES // CHUNK):
                rows = pl.ds(pl.multiple_of(i * LANES + s * CHUNK, CHUNK), CHUNK)
                side = side_depot[rows, :]
                total = None
                for j in range(n_h1):
                    keep = mask_one[i, j].astype(F32) * level_one[j]
                    value = body(rows, pl.ds(j * LANES, LANES), keep, side, lanes[j])
                    if rows_out:
                        total = value if total is None else total + value
                    if cols_out:
                        cols[j] = cols[j] + fold(value)
                if rows_out:
                    stage_depot[rows, :] = total
            return tuple(cols)

        zero = jnp.zeros((8, LANES), F32)
        cols = lax.fori_loop(0, n_d, block, (zero,) * n_h1 if cols_out else ())
        return [jnp.sum(v, axis=0, keepdims=True) for v in cols]

    def sweep_two(body, lanes, rows_out, cols_out):
        if cols_out:
            stage_zone[...] = jnp.zeros_like(stage_zone)

        def block(n, carry):
            i = n // (LANES // CHUNK)
            rows = pl.ds(pl.multiple_of(n * CHUNK, CHUNK), CHUNK)
            side = side_hub[rows, :]
            cap = side_cap[rows, :]

            def inner(j, total):
                cols = pl.ds(pl.multiple_of(j * LANES, LANES), LANES)
                keep = mask_two[i, j].astype(F32) * cap
                value = body(rows, cols, keep, side, lanes(j))
                if cols_out:
                    stage_zone[j] = stage_zone[j] + fold(value)
                return total + value if rows_out else total

            total = lax.fori_loop(0, n_z, inner, jnp.zeros((CHUNK, LANES), F32) if rows_out else 0)
            if rows_out:
                stage_hub[rows, :] = total
            return carry

        lax.fori_loop(0, n_h2 * (LANES // CHUNK), block, 0)

    def row_totals(stage, count):
        return [
            jnp.sum(jnp.transpose(stage[pl.ds(i * LANES, LANES), :]), axis=0, keepdims=True)
            for i in range(count)
        ]

    def send(t, hubs, cols_one):
        depot_rows = row_totals(stage_depot, n_d)
        for i in range(n_d):
            send_d[t, i : i + 1, :] = depot_rows[i]
        if hubs:
            hub_rows = row_totals(stage_hub, n_h2)
            for i in range(n_h2):
                send_d[t, n_d + i : n_d + i + 1, :] = hub_rows[i]
                send_z[t, n_z + n_h1 + i : n_z + n_h1 + i + 1, :] = hub_rows[i]
                send_h2[t, i // n_h1, i % n_h1 : i % n_h1 + 1, :] = hub_rows[i]
            for j in range(n_h1):
                send_d[t, n_d + n_h2 + j : n_d + n_h2 + j + 1, :] = cols_one[j]
                send_z[t, n_z + j : n_z + j + 1, :] = cols_one[j]
                send_h1[t, j : j + 1, :] = cols_one[j]
        send_z[t, 0:n_z, :] = jnp.sum(stage_zone[...], axis=1)
        if t == 0:
            pl.semaphore_wait(barrier, n_col * 2 + n_row * 3 - 2 - jnp.where(r == other, 2, 0))

        def put(src, dst, out_sem, in_sem, rr, cc):
            pltpu.make_async_remote_copy(
                src_ref=src,
                dst_ref=dst,
                send_sem=out_sem,
                recv_sem=in_sem,
                device_id=(rr, cc),
                device_id_type=MESH,
            ).start()

        if hubs:

            @pl.when(r != other)
            def _():
                loop(
                    n_col,
                    lambda k: put(
                        send_h1.at[t],
                        got_h1.at[t, r, lax.rem(c, 2)],
                        h1_out.at[t],
                        h1_in.at[t],
                        other,
                        lax.rem(c + k, n_col),
                    ),
                )

            for q in range(2):

                @pl.when(2 * r + q != c)
                def _():
                    loop(
                        n_row,
                        lambda k: put(
                            send_h2.at[t, q],
                            got_h2.at[t, c],
                            h2_out.at[t],
                            h2_in.at[t],
                            lax.rem(r + k, n_row),
                            2 * r + q,
                        ),
                    )

        loop(
            n_col - 1,
            lambda k: put(
                send_d.at[t], got_d.at[t, c], d_out.at[t], d_in.at[t], r, lax.rem(c + k + 1, n_col)
            ),
        )
        loop(
            n_row - 1,
            lambda k: put(
                send_z.at[t], got_z.at[t, r], z_out.at[t], z_in.at[t], lax.rem(r + k + 1, n_row), c
            ),
        )
        got_d[t, c] = send_d[t]
        got_z[t, r] = send_z[t]

    def arrived(ref, sem):
        pltpu.make_async_copy(ref, ref, sem).wait()

    def receive(t, hubs):
        arrived(got_d.at[t, pl.ds(0, n_col - 1)], d_in.at[t])
        arrived(got_z.at[t, pl.ds(0, n_row - 1)], z_in.at[t])
        all_d = jnp.sum(got_d[t], axis=0)
        all_z = jnp.sum(got_z[t], axis=0)
        depot_sum = all_d[0:n_d]
        zone_sum = all_z[0:n_z]
        if not hubs:
            return depot_sum, zone_sum, None, None
        arrived(got_h1.at[t, pl.ds(0, n_row - 1)], h1_in.at[t])
        arrived(got_h2.at[t, pl.ds(0, n_col - 1)], h2_in.at[t])
        for q in range(2):
            got_h1[t, r, q] = got_d[t, 2 * r + q, n_d + n_h2 : n_d + n_h2 + n_h1]
        start = n_z + n_h1

        @pl.when(lax.rem(c, 2) == 0)
        def _():
            got_h2[t, c] = got_z[t, other, start : start + n_h1]

        @pl.when(lax.rem(c, 2) == 1)
        def _():
            got_h2[t, c] = got_z[t, other, start + n_h1 : start + 2 * n_h1]

        one_here = all_z[n_z : n_z + n_h1] - jnp.sum(got_h2[t], axis=0)
        ones = jnp.sum(got_h1[t], axis=0)
        two_here = [
            ones[i // n_h1, i % n_h1 : i % n_h1 + 1] - all_d[n_d + i : n_d + i + 1] for i in range(n_h2)
        ]
        one_here = [one_here[j : j + 1] for j in range(n_h1)]
        return depot_sum, zone_sum, one_here, two_here

    def rows_of(value):
        return [value[i : i + 1] for i in range(value.shape[0])]

    hub_a = [hub_one(hub, j) for j in range(n_h1)]
    hub_b = [hub_two(hub, i) for i in range(n_h2)]
    depot_old = depot[...]
    zone_old = zone[...]
    set_sides(rows_of(0.25 * depot_old), [0.25 * v for v in hub_b])
    stage_lane = send_z.at[0]
    stage_lane[0:n_z, :] = 0.25 * zone_old

    def first_one(rows, cols, keep, side, lane):
        old = 0.5 * th1[rows, cols].astype(F32)
        cost = 0.25 * co1[rows, cols].astype(F32)
        new = old - cost - side - lane
        t_new = jnp.tanh(new)
        a1[rows, cols] = new - cost
        b1[rows, cols] = t_new
        return keep * (0.5 + t_new - 0.5 * jnp.tanh(old))

    def first_two(rows, cols, keep, side, lane):
        old = 0.5 * th2[rows, cols].astype(F32)
        cost = 0.25 * co2[rows, cols].astype(F32)
        new = old - cost + side + lane
        t_new = jnp.tanh(new)
        a2[rows, cols] = new - cost
        b2[rows, cols] = t_new
        return keep * (0.5 + t_new - 0.5 * jnp.tanh(old))

    def lane_rows(ref):
        return lambda j: ref[pl.ds(j, 1), :]

    bigs[0].wait()
    bigs[1].wait()
    cols_one = sweep_one(first_one, [0.25 * v for v in hub_a], True, True)
    bigs[2].wait()
    bigs[3].wait()
    sweep_two(first_two, lane_rows(stage_lane), True, True)
    send(0, True, cols_one)
    depot_sum, zone_sum, one_here, two_here = receive(0, True)

    supply_level = 0.5 * supply[...].astype(F32)
    demand_level = 0.125 * demand[...].astype(F32)
    grow_depot_0 = jnp.exp(STEP * (depot_sum * (1.0 / HUB) - supply_level))
    grow_zone_0 = jnp.exp(STEP * (demand_level - zone_sum * (1.0 / HUB)))
    depot_0 = depot_old * grow_depot_0
    zone_0 = zone_old * grow_zone_0
    hub_a = [v + s * (HUB_RATE / DEP) for v, s in zip(hub_a, one_here)]
    hub_b = [v + s * (HUB_RATE / DEP) for v, s in zip(hub_b, two_here)]

    set_sides(rows_of(0.25 * depot_0), [0.25 * v for v in hub_b])
    stage_lane = send_z.at[1]
    stage_lane[0:n_z, :] = 0.25 * zone_0

    def second_one(rows, cols, keep, side, lane):
        t_new = jnp.tanh(a1[rows, cols] - side - lane)
        a1[rows, cols] = t_new
        return keep * (0.5 + t_new - 0.5 * b1[rows, cols])

    def second_two(rows, cols, keep, side, lane):
        t_new = jnp.tanh(a2[rows, cols] + side + lane)
        a2[rows, cols] = t_new
        return keep * (0.5 + t_new - 0.5 * b2[rows, cols])

    sweep_one(second_one, [0.25 * v for v in hub_a], True, False)
    sweep_two(second_two, lane_rows(stage_lane), False, True)
    send(1, False, None)
    bigs[4].wait()
    bigs[5].wait()
    depot_sum, zone_sum, _, _ = receive(1, False)
    grow_depot_1 = jnp.exp(STEP * (depot_sum * (1.0 / HUB) - supply_level))
    grow_zone_1 = jnp.exp(STEP * (demand_level - zone_sum * (1.0 / HUB)))

    adj_depot = cot_depot[...]
    adj_zone = cot_zone[...]
    adj_a = [hub_one(cot_hub, j) for j in range(n_h1)]
    adj_b = [hub_two(cot_hub, i) for i in range(n_h2)]
    push_depot = adj_depot * (depot_0 * grow_depot_1) * (STEP / HUB)
    push_zone = -adj_zone * (zone_0 * grow_zone_1) * (STEP / HUB)
    set_sides(rows_of(push_depot), [-v * (HUB_RATE / DEP) for v in adj_b])
    stage_lane = send_z.at[2]
    stage_lane[0:n_z, :] = push_zone

    def third(ct, a, b, total_out, state_out):
        def body(rows, cols, keep, side, lane):
            weight = side + lane
            quarter = 0.25 * keep
            t_new = a[rows, cols]
            t_old = b[rows, cols]
            total = (quarter * (1.0 - t_new * t_new)) * (ct[rows, cols].astype(F32) + 2.0 * weight)
            slope_old = quarter * (1.0 - t_old * t_old)
            state = total - weight * slope_old
            b[rows, cols] = slope_old
            state_out[rows, cols] = state
            total_out[rows, cols] = -STEP * (total + state)
            return total

        return body

    cols_one = sweep_one(
        third(ct1, a1, b1, grad_cost_one, grad_one), [v * (HUB_RATE / DEP) for v in adj_a], True, True
    )
    sweep_two(third(ct2, a2, b2, grad_cost_two, grad_two), lane_rows(stage_lane), True, True)
    send(2, True, cols_one)

    def start_slope(th, a):
        def body(rows, cols, keep, side, lane):
            t_old = jnp.tanh(0.5 * th[rows, cols].astype(F32))
            a[rows, cols] = (0.25 * keep) * (1.0 - t_old * t_old)

        return body

    sweep_one(start_slope(th1, a1), [None] * n_h1, False, False)
    sweep_two(start_slope(th2, a2), lambda j: None, False, False)
    depot_sum, zone_sum, one_here, two_here = receive(2, True)
    adj_depot = adj_depot * grow_depot_1 - STEP * depot_sum
    adj_zone = adj_zone * grow_zone_1 + STEP * zone_sum
    adj_a = [v - STEP * s for v, s in zip(adj_a, one_here)]
    adj_b = [v - STEP * s for v, s in zip(adj_b, two_here)]

    push_depot = adj_depot * depot_0 * (STEP / HUB)
    push_zone = -adj_zone * zone_0 * (STEP / HUB)
    set_sides(rows_of(push_depot), [-v * (HUB_RATE / DEP) for v in adj_b])
    stage_lane = send_z.at[3]
    stage_lane[0:n_z, :] = push_zone

    def fourth(a, b, total_out, state_out):
        def body(rows, cols, keep, side, lane):
            weight = side + lane
            part = weight * b[rows, cols]
            total = state_out[rows, cols] + 2.0 * part
            state_out[rows, cols] = total - weight * a[rows, cols]
            total_out[rows, cols] = total_out[rows, cols] - part
            return total

        return body

    cols_one = sweep_one(
        fourth(a1, b1, grad_cost_one, grad_one), [v * (HUB_RATE / DEP) for v in adj_a], True, True
    )
    sweep_two(fourth(a2, b2, grad_cost_two, grad_two), lane_rows(stage_lane), True, True)
    send(3, True, cols_one)
    depot_sum, zone_sum, one_here, two_here = receive(3, True)
    grad_depot[...] = adj_depot * grow_depot_0 - STEP * depot_sum
    grad_zone[...] = adj_zone * grow_zone_0 + STEP * zone_sum
    for i in range(n_h2):
        got_g[r, i : i + 1, :] = adj_b[i] - STEP * two_here[i]

    def give(k):
        pltpu.make_async_remote_copy(
            src_ref=got_g.at[r],
            dst_ref=got_g.at[r],
            send_sem=g_out.at[0],
            recv_sem=g_in.at[0],
            device_id=(lax.rem(r + k + 1, n_row), c),
            device_id_type=MESH,
        ).start()

    loop(n_row - 1, give)
    arrived(got_g.at[pl.ds(0, n_row - 1)], g_in.at[0])
    for k in range(n_row):
        grad_hub[k * n_h2 : (k + 1) * n_h2, :] = got_g[k]

    arrived(got_g.at[pl.ds(0, n_row - 1)], g_out.at[0])
    for t in range(4):
        arrived(got_d.at[t, pl.ds(0, n_col - 1)], d_out.at[t])
        arrived(got_z.at[t, pl.ds(0, n_row - 1)], z_out.at[t])
        if t != 1:

            @pl.when(r != other)
            def _():
                arrived(got_h2.at[t], h1_out.at[t])
                arrived(got_h2.at[t], h2_out.at[t])

            @pl.when(r == other)
            def _():
                arrived(got_h2.at[t, pl.ds(0, n_row)], h2_out.at[t])


def on_device(n_row, n_col, *args):
    (theta_one, theta_two, cost_one, cost_two, depot, hub, zone, mask_one, mask_two) = args[:9]
    (supply, demand, capacity, cot_one, cot_two, cot_depot, cot_hub, cot_zone) = args[9:]

    def packed(vector):
        return vector.reshape(vector.shape[0] // LANES, LANES)

    depots, hubs_one = theta_one.shape
    hubs_two, zones = theta_two.shape
    n_d, n_z, n_h = depots // LANES, zones // LANES, hub.shape[0] // LANES
    n_h1, n_h2 = hubs_one // LANES, hubs_two // LANES
    rows_d = -(-(n_d + n_h1 + n_h2) // 8) * 8
    rows_z = -(-(n_z + n_h1 + n_h2) // 8) * 8
    big_one, big_two = (depots, hubs_one), (hubs_two, zones)
    any_spec = pl.BlockSpec(memory_space=pl.ANY)
    smem = pl.BlockSpec(memory_space=pltpu.SMEM)
    vmem = pl.BlockSpec(memory_space=pltpu.VMEM)
    dma = pltpu.SemaphoreType.DMA
    in_specs = [any_spec] * 7 + [smem] * 2 + [any_spec] * 8
    outs = pl.pallas_call(
        functools.partial(kernel, n_row, n_col),
        out_shape=[
            jax.ShapeDtypeStruct(big_one, F32),
            jax.ShapeDtypeStruct(big_two, F32),
            jax.ShapeDtypeStruct(big_one, F32),
            jax.ShapeDtypeStruct(big_two, F32),
            jax.ShapeDtypeStruct((n_d, LANES), F32),
            jax.ShapeDtypeStruct((n_h, LANES), F32),
            jax.ShapeDtypeStruct((n_z, LANES), F32),
        ],
        in_specs=in_specs,
        out_specs=[vmem] * 7,
        scratch_shapes=[
            pltpu.VMEM(big_one, jnp.bfloat16),
            pltpu.VMEM(big_two, jnp.bfloat16),
            pltpu.VMEM(big_one, jnp.bfloat16),
            pltpu.VMEM(big_two, jnp.bfloat16),
            pltpu.VMEM(big_one, jnp.bfloat16),
            pltpu.VMEM(big_two, jnp.bfloat16),
            pltpu.VMEM((n_d, LANES), F32),
            pltpu.VMEM((n_h, LANES), F32),
            pltpu.VMEM((n_z, LANES), F32),
            pltpu.VMEM((n_d, LANES), jnp.int32),
            pltpu.VMEM((n_z, LANES), jnp.int32),
            pltpu.VMEM((n_h, LANES), jnp.int32),
            pltpu.VMEM((n_d, LANES), F32),
            pltpu.VMEM((n_h, LANES), F32),
            pltpu.VMEM((n_z, LANES), F32),
            pltpu.VMEM(big_one, F32),
            pltpu.VMEM(big_two, F32),
            pltpu.VMEM(big_one, F32),
            pltpu.VMEM(big_two, F32),
            pltpu.VMEM((depots, LANES), F32),
            pltpu.VMEM((hubs_two, LANES), F32),
            pltpu.VMEM((hubs_two, LANES), F32),
            pltpu.VMEM((depots, LANES), F32),
            pltpu.VMEM((hubs_two, LANES), F32),
            pltpu.VMEM((n_z, 8, LANES), F32),
            pltpu.VMEM((4, rows_d, LANES), F32),
            pltpu.VMEM((4, rows_z, LANES), F32),
            pltpu.VMEM((4, n_h1, LANES), F32),
            pltpu.VMEM((4, 2, n_h1, LANES), F32),
            pltpu.VMEM((4, n_col, rows_d, LANES), F32),
            pltpu.VMEM((4, n_row, rows_z, LANES), F32),
            pltpu.VMEM((4, n_row, 2, n_h1, LANES), F32),
            pltpu.VMEM((4, n_col, n_h1, LANES), F32),
            pltpu.VMEM((n_row, n_h2, LANES), F32),
            dma((6,)),
            dma((9,)),
            dma((4,)),
            dma((4,)),
            dma((4,)),
            dma((4,)),
            dma((4,)),
            dma((4,)),
            dma((4,)),
            dma((4,)),
            dma((1,)),
            dma((1,)),
        ],
        compiler_params=pltpu.CompilerParams(
            collective_id=0, has_side_effects=True, vmem_limit_bytes=60 * 1024 * 1024
        ),
    )(
        theta_one,
        theta_two,
        cost_one,
        cost_two,
        packed(depot),
        packed(hub),
        packed(zone),
        mask_one,
        mask_two,
        packed(supply),
        packed(demand),
        packed(capacity),
        cot_one,
        cot_two,
        packed(cot_depot),
        packed(cot_hub),
        packed(cot_zone),
    )
    return tuple(outs[:4]) + tuple(v.reshape(-1) for v in outs[4:])


def solution(mesh):
    n_row, n_col = mesh.shape["row"], mesh.shape["col"]
    block, by_row, by_col = P("row", "col"), P("row"), P("col")
    return jax.shard_map(
        functools.partial(on_device, n_row, n_col),
        mesh=mesh,
        in_specs=(
            (block,) * 4 + (by_row, P(), by_col, block, block, by_row, by_col, P(), block, block)
            + (by_row, P(), by_col)
        ),
        out_specs=(block,) * 4 + (by_row, P(), by_col),
        check_vma=False,
    )
```

time: 392 us -> 71.1 us (0.18)
  blocking collectives: 340 us -> 0 us
  Pallas kernels: 0 us -> 57 us
  other arithmetic: 46.9 us -> 0 us
  local copies, waits for them, and re-layouts: 3.04 us -> 13.3 us
    psum x8 -> x0, blocking collectives: 210 us -> none  [the longest x4 152 us: dual_sums(): depot_sum, hub_two_sum = lax.psum((depot_part, hub_two_part), 'col')]
    all_gather x6 -> x0, blocking collectives: 131 us -> none  [the longest x3 73.2 us: dual_sums(): lax.all_gather(hub_one_sum, 'col', axis=0, tiled=True)]
    pallas_call x0 -> x1, Pallas kernels: none -> 57 us  [on_device(): pl.pallas_call(functools.partial(kernel, n_row, n_col), out_shape=[jax.Sh...]
    reduce_sum x8 -> x0, other arithmetic: 33.8 us -> none  [the longest x2 14 us: on_device(): jnp.sum(total_two, axis=0)]
    unnamed x32 -> x18, local copies, waits for them, and re-layouts: 0.09 us -> 13.3 us
    sub x3 -> x0, other arithmetic: 8.74 us -> none  [the longest x1 6.23 us: on_device(): grad_second = grad_second - STEP_PRIMAL * total_two]
where the time goes in v1:
time: 71.1 us; the launch traced here: 70.9 us
  Pallas kernels  57 us (80%)
  local copies, waits for them, and re-layouts  13.3 us (19%)
    pallas_call x1, Pallas kernels, on_device(): pl.pallas_call(functools.partial(kernel, n_row, n_col), out_shape=[jax.Sh...  57 us
    unnamed x18, local copies, waits for them, and re-layouts  13.3 us

profile of v1, /device:TPU:1, one launch (start us, length us, event | category | flops | bytes accessed | tf_op | source)
XLA Modules:
  0.0 70.9 jit_solution(16829212652822780318)
XLA Ops:
  0.6 1.3 %copy.24.mask_one = s32[8,2]{1,0:T(8,128)} copy(s32[8,2]{0,1:T(2,128)} %param.24) | data formatting | bytes 128 | tf_op args[7]
  2.0 57.0 %shard_map.216 = (f32[1024,256]{1,0:T(8,128)}, f32[512,2048]{1,0:T(8,128)}, f32[1024,256]{1,0:T(8,128)}, f32[512,2048]{1,0:T(8,128)}, f32[8,128]{1,0:T(8,128)}, /*index=5*/f32[32,128]{1,0:T(8,128)}, f32[16,128]{1,0:T(8,128)}) custom-call(bf16[1024,256]{1,0:T(8,128)(2,1)} %theta_one.1, bf16[512,2048]{1,0:T(8,128)(2,1)} %theta_two.1, ...), custom_call_target="tpu_custom_call" | custom-call | tf_op jit(solution)/shard_map/pallas_call | solution.py:549
  59.0 2.3 %copy.32 = f32[1024,256]{1,0:T(8,128)} copy(f32[1024,256]{1,0:T(8,128)} %get-tuple-element.28) | data formatting | bytes 2097152
  61.2 0.0 copy-start.1
  61.2 0.0 copy-start
  61.2 4.8 %copy.33 = f32[512,2048]{1,0:T(8,128)} copy(f32[512,2048]{1,0:T(8,128)} %get-tuple-element.29) | data formatting | bytes 8388608
  66.1 0.0 copy-done.1
  66.1 1.0 %copy.34 = f32[1024,256]{1,0:T(8,128)} copy(f32[1024,256]{1,0:T(8,128)S(1)} %copy-done.1) | data formatting | bytes 2097152
  67.0 0.0 copy-done
  67.0 0.0 copy-start.4
  67.1 0.0 copy-start.2
  67.1 0.0 copy-start.3
  67.1 2.0 %copy.35 = f32[512,2048]{1,0:T(8,128)} copy(f32[512,2048]{1,0:T(8,128)S(1)} %copy-done) | data formatting | bytes 8388608
  69.1 0.0 copy-done.4
  69.1 0.6 copy.36
  69.7 0.0 copy-done.2
  69.7 0.6 copy.37
  70.3 0.0 copy-done.3
  70.3 0.6 copy.38
Async XLA Ops:
  61.2 4.9 %copy-start.1 = (f32[1024,256]{1,0:T(8,128)S(1)}, f32[1024,256]{1,0:T(8,128)}, u32[]{:S(2)}) copy-start(f32[1024,256]{1,0:T(8,128)} %get-tuple-element.30) | copy-start | bytes 3145732
  61.2 5.8 %copy-start = (f32[512,2048]{1,0:T(8,128)S(1)}, f32[512,2048]{1,0:T(8,128)}, u32[]{:S(2)}) copy-start(f32[512,2048]{1,0:T(8,128)} %get-tuple-element.31) | copy-start | bytes 12582916
  67.0 2.0 %copy-start.4 = (f32[8,128]{1,0:T(8,128)S(1)}, f32[8,128]{1,0:T(8,128)}, u32[]{:S(2)}) copy-start(f32[8,128]{1,0:T(8,128)} %get-tuple-element.18) | copy-start | bytes 12292
  67.1 2.6 %copy-start.2 = (f32[32,128]{1,0:T(8,128)S(1)}, f32[32,128]{1,0:T(8,128)}, u32[]{:S(2)}) copy-start(f32[32,128]{1,0:T(8,128)} %get-tuple-element.19) | copy-start | bytes 49156
  67.1 3.2 %copy-start.3 = (f32[16,128]{1,0:T(8,128)S(1)}, f32[16,128]{1,0:T(8,128)}, u32[]{:S(2)}) copy-start(f32[16,128]{1,0:T(8,128)} %get-tuple-element.20) | copy-start | bytes 24580

commit v2 on v0

v2 whole, which is shorter than its diff:
```python
import functools
import types

import jax
import jax.numpy as jnp
from jax import lax
from jax.experimental import pallas as pl
from jax.experimental.pallas import tpu as pltpu
from jax.sharding import PartitionSpec as P

DEP = 8192
HUB = 4096
LANES = 128
STEP = 0.5
HUB_RATE = 4.0
CHUNK = 32
WIDE = 16
MESH = pl.DeviceIdType.MESH
F32 = jnp.float32
FIRST, SECOND, LINEAR, THIRD, FINAL_HUB, FOURTH = range(6)


def fold(values):
    return jnp.sum(values.reshape(values.shape[0] // 8, 8, LANES), axis=0)


def spread(row):
    return jnp.transpose(jnp.broadcast_to(row, (LANES, LANES)))


def loop(count, body):
    def step(k, carry):
        body(k)
        return carry

    lax.fori_loop(0, count, step, 0)


def arrived(ref, sem):
    pltpu.make_async_copy(ref, ref, sem).wait()


def main_kernel(n_row, n_col, n_in, n_out, tree, *refs):
    (theta_one, theta_two, cost_one, cost_two, depot_hbm, hub_hbm, zone_hbm, mask_one_hbm, mask_two_hbm) = refs[:9]
    (supply_hbm, demand_hbm, capacity_hbm, cot_one, cot_two) = refs[9:14]
    (cot_depot_hbm, cot_hub_hbm, cot_zone_hbm) = refs[14:17]
    (grad_one, grad_two, grad_cost_one, grad_cost_two, grad_depot, grad_hub, grad_zone) = refs[n_in : n_in + n_out]
    m = types.SimpleNamespace(**jax.tree.unflatten(tree, refs[n_in + n_out :]))

    r = lax.axis_index("row")
    c = lax.axis_index("col")
    other = c // 2
    n_d = m.depot.shape[0]
    n_z = m.zone.shape[0]
    n_h1 = theta_one.shape[1] // LANES
    n_h2 = theta_two.shape[0] // LANES
    halves = LANES // CHUNK

    def load(src, dst, sem):
        copy = pltpu.make_async_copy(src, dst, sem)
        copy.start()
        return copy

    mask_one, mask_two = m.mask_one, m.mask_two
    pairs = (
        (depot_hbm, m.depot),
        (capacity_hbm, m.capacity),
        (hub_hbm, m.hub),
        (zone_hbm, m.zone),
        (mask_one_hbm, mask_one),
        (mask_two_hbm, mask_two),
    )
    smalls = [load(src, dst, m.small_sem.at[n]) for n, (src, dst) in enumerate(pairs)]
    loads_one = [load(theta_one, m.th1, m.load_sem.at[0]), load(cost_one, m.co1, m.load_sem.at[1])]

    def load_two(i):
        rows = pl.ds(i * LANES, LANES)
        pairs = ((theta_two, m.th2), (cost_two, m.co2))
        return [load(src.at[rows], dst.at[rows], m.two_sem.at[i, n]) for n, (src, dst) in enumerate(pairs)]

    early = n_h2 // 2
    loads_two = [load_two(i) for i in range(early)]

    barrier = pltpu.get_barrier_semaphore()

    def signal(rr, cc):
        pl.semaphore_signal(barrier, inc=1, device_id=(rr, cc), device_id_type=MESH)

    @pl.when(r != other)
    def _():
        loop(n_col, lambda k: signal(other, lax.rem(c + k, n_col)))
        for q in range(2):
            loop(n_row, lambda k: signal(lax.rem(r + k, n_row), 2 * r + q))

    @pl.when(r == other)
    def _():
        loop(n_col - 1, lambda k: signal(r, lax.rem(c + k + 1, n_col)))
        loop(n_row - 1, lambda k: signal(lax.rem(r + k + 1, n_row), c))
        loop(n_row, lambda k: signal(lax.rem(r + k, n_row), c + 1 - 2 * lax.rem(c, 2)))

    loop(n_col - 1, lambda k: signal(r, lax.rem(c + k + 1, n_col)))
    loop(n_row - 1, lambda k: signal(lax.rem(r + k + 1, n_row), c))

    for copy in smalls:
        copy.wait()

    def hub_one(ref):
        return jnp.concatenate([ref[pl.ds(c * n_h1 + j, 1), :] for j in range(n_h1)], axis=0)

    def hub_two(ref):
        return jnp.concatenate([ref[pl.ds(r * n_h2 + i, 1), :] for i in range(n_h2)], axis=0)

    def set_side(ref, packed):
        for i in range(packed.shape[0]):
            ref[i * LANES : (i + 1) * LANES, :] = spread(packed[i : i + 1])

    level_one = hub_one(m.capacity).astype(F32)
    set_side(m.side_cap, 0.25 * hub_two(m.capacity).astype(F32))

    def sweep_one(body, n_rows, n_cols):
        def block(i, cols):
            cols = list(cols)
            writes = []
            totals = []
            for s in range(halves):
                rows = pl.ds(pl.multiple_of(i * LANES + s * CHUNK, CHUNK), CHUNK)
                total = [None] * n_rows
                for j in range(n_h1):
                    keep = mask_one[j, i].astype(F32) * level_one[j : j + 1]
                    lanes = pl.ds(j * LANES, LANES)
                    by_row, by_col, stores = body(rows, lanes, keep, j)
                    for n, value in enumerate(by_row):
                        total[n] = value if total[n] is None else total[n] + value
                    for n, value in enumerate(by_col):
                        cols[n * n_h1 + j] = cols[n * n_h1 + j] + fold(value)
                    writes += [(ref, rows, lanes, value) for ref, value in stores]
                totals.append((rows, total))
            for ref, rows, lanes, value in writes:
                ref[rows, lanes] = value
            for rows, total in totals:
                for n in range(n_rows):
                    m.stage_depot[n, rows, :] = total[n]
            return tuple(cols)

        zero = jnp.zeros((8, LANES), F32)
        cols = lax.fori_loop(0, n_d, block, (zero,) * (n_h1 * n_cols))
        cols = [jnp.sum(v, axis=0, keepdims=True) for v in cols]
        return [jnp.concatenate(cols[n * n_h1 : (n + 1) * n_h1], axis=0) for n in range(n_cols)]

    def sweep_two(body, n_rows, n_cols, before=None):
        for n in range(n_cols):
            m.stage_zone[n] = jnp.zeros(m.stage_zone.shape[1:], F32)

        def block(n, i):
            rows = pl.ds(pl.multiple_of(n * CHUNK, CHUNK), CHUNK)
            cap = m.side_cap[rows, :]

            def inner(jj, totals):
                totals = list(totals)
                writes = []
                for q in range(WIDE):
                    j = jj * WIDE + q
                    lanes = pl.ds(pl.multiple_of(j * LANES, LANES), LANES)
                    keep = mask_two[i, j].astype(F32) * cap
                    by_row, by_col, stores = body(rows, lanes, keep, j)
                    for k, value in enumerate(by_row):
                        totals[k] = totals[k] + value
                    writes += [(m.stage_zone, (k, j), fold(value)) for k, value in enumerate(by_col)]
                    writes += [(ref, (rows, lanes), value) for ref, value in stores]
                for ref, where, value in writes:
                    if ref is m.stage_zone:
                        value = ref[where] + value
                    ref[where] = value
                return tuple(totals)

            zero = jnp.zeros((CHUNK, LANES), F32)
            totals = lax.fori_loop(0, n_z // WIDE, inner, (zero,) * n_rows)
            for k in range(n_rows):
                m.stage_hub[k, rows, :] = totals[k]

        if before is None:
            loop(n_h2 * halves, lambda n: block(n, n // halves))
        else:
            for i in range(n_h2):
                before(i)
                loop(halves, lambda s: block(i * halves + s, i))

    def packed_rows(stage, n, count):
        parts = [
            jnp.sum(jnp.transpose(stage[n, i * LANES : (i + 1) * LANES, :]), axis=0, keepdims=True)
            for i in range(count)
        ]
        return jnp.concatenate(parts, axis=0)

    def depot_rows(n):
        return packed_rows(m.stage_depot, n, n_d)

    def hub_rows(n):
        return packed_rows(m.stage_hub, n, n_h2)

    def zone_cols(n):
        return jnp.sum(m.stage_zone[n], axis=1)

    def fill(ref, *parts):
        start = 0
        for part in parts:
            ref[start : start + part.shape[0], :] = part
            start += part.shape[0]

    def put(src, dst, out_sem, in_sem, rr, cc):
        pltpu.make_async_remote_copy(
            src_ref=src,
            dst_ref=dst,
            send_sem=out_sem,
            recv_sem=in_sem,
            device_id=(rr, cc),
            device_id_type=MESH,
        ).start()

    def share_cols(t):
        src, got = m.send_d[t], m.got_d[t]
        sems = m.d_out.at[t], m.d_in.at[t]
        loop(n_col - 1, lambda k: put(src, got.at[c], *sems, r, lax.rem(c + k + 1, n_col)))
        got[c] = src[...]

    def share_rows(t):
        src, got = m.send_z[t], m.got_z[t]
        sems = m.z_out.at[t], m.z_in.at[t]
        loop(n_row - 1, lambda k: put(src, got.at[r], *sems, lax.rem(r + k + 1, n_row), c))
        got[r] = src[...]

    def share_one(t):
        sems = m.h1_out.at[t], m.h1_in.at[t]

        @pl.when(r != other)
        def _():
            loop(
                n_col,
                lambda k: put(
                    m.send_h1[t],
                    m.got_h1[t].at[r, lax.rem(c, 2)],
                    *sems,
                    other,
                    lax.rem(c + k, n_col),
                ),
            )

    def share_two(t):
        sems = m.h2_out.at[t], m.h2_in.at[t]
        for q in range(2):

            @pl.when(2 * r + q != c)
            def _():
                loop(
                    n_row,
                    lambda k: put(
                        m.send_h2[t].at[q], m.got_h2[t].at[c], *sems, lax.rem(r + k, n_row), 2 * r + q
                    ),
                )

    def from_cols(t):
        got = m.got_d[t]
        arrived(got.at[pl.ds(0, n_col - 1)], m.d_in.at[t])
        return jnp.sum(got[...], axis=0)

    def from_rows(t):
        got = m.got_z[t]
        arrived(got.at[pl.ds(0, n_row - 1)], m.z_in.at[t])
        return jnp.sum(got[...], axis=0)

    def send_hubs(t, one, two, lead_d, lead_z):
        fill(m.send_h1[t], one)
        for q in range(2):
            m.send_h2[t][q] = two[q * n_h1 : (q + 1) * n_h1]
        fill(m.send_d[t], *lead_d, two, one)
        fill(m.send_z[t], *lead_z, one, two)

    def receive_one(t, start):
        got = m.got_h1[t]
        size = got.shape[2]
        arrived(got.at[pl.ds(0, n_row - 1)], m.h1_in.at[t])
        for q in range(2):
            got[r, q] = m.got_d[t][2 * r + q, start : start + size]
        return jnp.sum(got[...], axis=0)

    def receive_two(t, start):
        got = m.got_h2[t]
        arrived(got.at[pl.ds(0, n_col - 1)], m.h2_in.at[t])
        for q in range(2):

            @pl.when(lax.rem(c, 2) == q)
            def _():
                got[c] = m.got_z[t][other, start + q * n_h1 : start + (q + 1) * n_h1]

        return jnp.sum(got[...], axis=0)

    def receive_hubs(t, all_d, all_z, lead_d, lead_z):
        ones = receive_one(t, lead_d + n_h2)
        one_here = all_z[lead_z : lead_z + n_h1] - receive_two(t, lead_z + n_h1)
        ones = jnp.concatenate([ones[0], ones[1]], axis=0)
        return one_here, ones - all_d[lead_d : lead_d + n_h2]

    hub_a = hub_one(m.hub)
    hub_b = hub_two(m.hub)
    depot_old = m.depot[...]
    zone_old = m.zone[...]
    set_side(m.side_depot, 0.25 * depot_old)
    set_side(m.side_hub, 0.25 * hub_b)
    m.lane_zone[0] = 0.25 * zone_old
    lane_one = 0.25 * hub_a

    def first(th, co, a, b, z, sign, weights):
        def body(rows, lanes, keep, j):
            old = 0.5 * th[rows, lanes].astype(F32)
            cost = 0.25 * co[rows, lanes].astype(F32)
            new = old - cost + sign * weights(rows, j)
            t_old = jnp.tanh(old)
            t_new = jnp.tanh(new)
            value = keep * (0.5 + t_new - 0.5 * t_old)
            return [value], [value], [(a, new - cost), (b, t_new), (z, t_old)]

        return body

    for copy in loads_one:
        copy.wait()
    loads_two += [load_two(i) for i in range(early, n_h2)]
    (one,) = sweep_one(
        first(
            m.th1,
            m.co1,
            m.a1,
            m.b1,
            m.z1,
            -1.0,
            lambda rows, j: m.side_depot[rows, :] + lane_one[j : j + 1],
        ),
        1,
        1,
    )

    def zone_lane(k, j):
        return m.lane_zone[k, pl.ds(j, 1), :]

    def wait_two(i):
        for copy in loads_two[i]:
            copy.wait()

    sweep_two(
        first(
            m.th2,
            m.co2,
            m.a2,
            m.b2,
            m.z2,
            1.0,
            lambda rows, j: m.side_hub[rows, :] + zone_lane(0, j),
        ),
        1,
        1,
        wait_two,
    )
    pairs = (
        (cot_depot_hbm, m.cot_depot),
        (cot_hub_hbm, m.cot_hub),
        (cot_zone_hbm, m.cot_zone),
        (supply_hbm, m.supply),
        (demand_hbm, m.demand),
    )
    smalls = [load(src, dst, m.small_sem.at[n + 6]) for n, (src, dst) in enumerate(pairs)]
    late = [load(cot_one, m.ct1, m.load_sem.at[2]), load(cot_two, m.ct2, m.load_sem.at[3])]
    send_hubs(FIRST, one, hub_rows(0), [depot_rows(0)], [zone_cols(0)])
    pl.semaphore_wait(barrier, n_col * 2 + n_row * 3 - 2 - jnp.where(r == other, 2, 0))
    share_one(FIRST)
    share_two(FIRST)
    share_cols(FIRST)
    share_rows(FIRST)

    for copy in smalls:
        copy.wait()
    adj_depot = m.cot_depot[...]
    adj_zone = m.cot_zone[...]
    adj_a = hub_one(m.cot_hub)
    adj_b = hub_two(m.cot_hub)
    push_a = adj_a * (HUB_RATE / DEP)
    push_b = adj_b * (-HUB_RATE / DEP)
    set_side(m.side_push, push_b)
    supply_level = 0.5 * m.supply[...].astype(F32)
    demand_level = 0.125 * m.demand[...].astype(F32)

    def slopes(b, z, keep, rows, lanes):
        t_new = b[rows, lanes]
        t_old = z[rows, lanes]
        quarter = 0.25 * keep
        square = t_new * t_new
        rest = 1.0 - square
        slope = quarter * rest
        return keep * (0.5 - 0.5 * t_new), slope, quarter * (rest - square + t_old * t_old)

    def window_one(rows, lanes, keep, j):
        past, slope, mixed = slopes(m.b1, m.z1, keep, rows, lanes)
        return [past, slope, slope * push_a[j : j + 1]], [slope], [(m.b1, slope), (m.z1, mixed)]

    def window_two(rows, lanes, keep, j):
        past, slope, mixed = slopes(m.b2, m.z2, keep, rows, lanes)
        return [slope], [past, slope, slope * m.side_push[rows, :]], [(m.b2, slope), (m.z2, mixed)]

    (slope_a,) = sweep_one(window_one, 3, 1)
    past_depot, slope_depot, pushed_depot = depot_rows(0), depot_rows(1), depot_rows(2)
    sweep_two(window_two, 1, 3)
    past_zone, slope_zone, pushed_zone = zone_cols(0), zone_cols(1), zone_cols(2)
    slope_b = hub_rows(0)

    all_d = from_cols(FIRST)
    all_z = from_rows(FIRST)
    one_here, two_here = receive_hubs(FIRST, all_d, all_z, n_d, n_z)
    grow_depot_0 = jnp.exp(STEP * (all_d[0:n_d] * (1.0 / HUB) - supply_level))
    grow_zone_0 = jnp.exp(STEP * (demand_level - all_z[0:n_z] * (1.0 / HUB)))
    depot_0 = depot_old * grow_depot_0
    zone_0 = zone_old * grow_zone_0
    hub_a = hub_a + one_here * (HUB_RATE / DEP)
    hub_b = hub_b + two_here * (HUB_RATE / DEP)

    set_side(m.side_depot, 0.25 * depot_0)
    set_side(m.side_hub, 0.25 * hub_b)
    m.lane_zone[0] = 0.25 * zone_0
    lane_one_next = 0.25 * hub_a

    def second_one(rows, lanes, keep, j):
        t_new = jnp.tanh(m.a1[rows, lanes] - (m.side_depot[rows, :] + lane_one_next[j : j + 1]))
        return [keep * t_new], [], [(m.a1, t_new)]

    def second_two(rows, lanes, keep, j):
        t_new = jnp.tanh(m.a2[rows, lanes] + (m.side_hub[rows, :] + zone_lane(0, j)))
        return [], [keep * t_new], [(m.a2, t_new)]

    sweep_one(second_one, 1, 0)
    sweep_two(second_two, 0, 1)
    fill(m.send_d[1], depot_rows(0) + past_depot)
    fill(m.send_z[1], zone_cols(0) + past_zone)
    share_cols(SECOND)
    share_rows(SECOND)

    for copy in late:
        copy.wait()

    def linear_one(rows, lanes, keep, j):
        t_new = m.a1[rows, lanes]
        beta = (0.25 * keep) * (1.0 - t_new * t_new)
        alpha = beta * (m.ct1[rows, lanes].astype(F32) + 2.0 * push_a[j : j + 1])
        return [alpha, beta], [alpha], [(m.a1, beta), (m.w1, alpha)]

    def linear_two(rows, lanes, keep, j):
        t_new = m.a2[rows, lanes]
        beta = (0.25 * keep) * (1.0 - t_new * t_new)
        alpha = beta * (m.ct2[rows, lanes].astype(F32) + 2.0 * m.side_push[rows, :])
        return [alpha], [alpha, beta], [(m.a2, beta), (m.w2, alpha)]

    (alpha_a,) = sweep_one(linear_one, 2, 1)
    alpha_depot, beta_depot = depot_rows(0), depot_rows(1)
    sweep_two(linear_two, 1, 2)
    alpha_zone, beta_zone = zone_cols(0), zone_cols(1)
    alpha_b = hub_rows(0)
    fill(m.send_d[2], alpha_depot, beta_depot)
    fill(m.send_z[2], alpha_zone, beta_zone)
    share_cols(LINEAR)
    share_rows(LINEAR)

    grow_depot_1 = jnp.exp(STEP * (from_cols(SECOND) * (1.0 / HUB) - supply_level))
    grow_zone_1 = jnp.exp(STEP * (demand_level - from_rows(SECOND) * (1.0 / HUB)))

    push_depot = adj_depot * (depot_0 * grow_depot_1) * (STEP / HUB)
    push_zone = -adj_zone * (zone_0 * grow_zone_1) * (STEP / HUB)
    set_side(m.side_depot, 2.0 * push_depot)
    m.lane_zone[0] = 2.0 * push_zone

    def third_one(rows, lanes, keep, j):
        return [], [m.a1[rows, lanes] * m.side_depot[rows, :]], []

    def third_two(rows, lanes, keep, j):
        return [m.a2[rows, lanes] * zone_lane(0, j)], [], []

    (one,) = sweep_one(third_one, 0, 1)
    sweep_two(third_two, 1, 0)
    one = one + alpha_a
    two = hub_rows(0) + alpha_b
    send_hubs(THIRD, one, two, [], [])
    share_one(THIRD)
    share_two(THIRD)
    share_cols(THIRD)
    share_rows(THIRD)

    all_d = from_cols(LINEAR)
    all_z = from_rows(LINEAR)
    adj_depot = adj_depot * grow_depot_1 - STEP * (all_d[0:n_d] + 2.0 * push_depot * all_d[n_d : 2 * n_d])
    adj_zone = adj_zone * grow_zone_1 + STEP * (all_z[0:n_z] + 2.0 * push_zone * all_z[n_z : 2 * n_z])
    last_depot = adj_depot * depot_0 * (STEP / HUB)
    last_zone = -adj_zone * zone_0 * (STEP / HUB)
    set_side(m.side_last, last_depot)
    m.lane_zone[1] = last_zone

    def both_one(rows, lanes, keep, j):
        weight = 2.0 * m.side_last[rows, :] - 0.5 * m.side_depot[rows, :]
        return [], [m.b1[rows, lanes] * weight], []

    def both_two(rows, lanes, keep, j):
        return [m.b2[rows, lanes] * (2.0 * zone_lane(1, j) - 0.5 * zone_lane(0, j))], [], []

    (more,) = sweep_one(both_one, 0, 1)
    one = one + more - push_a * slope_a
    sweep_two(both_two, 1, 0)
    two = two + hub_rows(0) - push_b * slope_b
    fill(m.send_h1[4], one, slope_a)
    fill(m.send_d[4], two, slope_b, one, slope_a)
    share_one(FINAL_HUB)
    share_cols(FINAL_HUB)

    def state(total, weight, last, slope, mixed):
        part = weight * slope
        return total - part + last * mixed, 0.5 * part - total - last * slope

    def state_one(rows, lanes, keep, j):
        twice = m.side_depot[rows, :]
        total = m.w1[rows, lanes] + twice * m.a1[rows, lanes]
        weight = 0.5 * twice + push_a[j : j + 1]
        theta, cost = state(
            total, weight, m.side_last[rows, :], m.b1[rows, lanes], m.z1[rows, lanes]
        )
        return [], [], [(grad_one, theta), (grad_cost_one, cost)]

    def state_two(rows, lanes, keep, j):
        twice = zone_lane(0, j)
        total = m.w2[rows, lanes] + twice * m.a2[rows, lanes]
        weight = 0.5 * twice + m.side_push[rows, :]
        theta, cost = state(total, weight, zone_lane(1, j), m.b2[rows, lanes], m.z2[rows, lanes])
        return [], [], [(grad_two, theta), (grad_cost_two, cost)]

    sweep_one(state_one, 0, 0)
    sweep_two(state_two, 0, 0)

    all_d = from_cols(THIRD)
    all_z = from_rows(THIRD)
    one_here, two_here = receive_hubs(THIRD, all_d, all_z, 0, 0)
    adj_a = adj_a - STEP * one_here
    adj_b = adj_b - STEP * two_here
    last_a = adj_a * (HUB_RATE / DEP)
    last_b = adj_b * (-HUB_RATE / DEP)

    set_side(m.side_hub, last_b)

    def fourth_one(rows, lanes, keep, j):
        return [m.b1[rows, lanes] * last_a[j : j + 1]], [], []

    def fourth_two(rows, lanes, keep, j):
        return [], [m.b2[rows, lanes] * m.side_hub[rows, :]], []

    sweep_one(fourth_one, 1, 0)
    sweep_two(fourth_two, 0, 1)

    def last_sum(alpha, beta, push, slope, pushed, last, value):
        return alpha + 2.0 * push * beta + (2.0 * last - push) * slope - pushed + 2.0 * value

    fill(
        m.send_d[5],
        last_sum(alpha_depot, beta_depot, push_depot, slope_depot, pushed_depot, last_depot, depot_rows(0)),
    )
    fill(
        m.send_z[5],
        last_sum(alpha_zone, beta_zone, push_zone, slope_zone, pushed_zone, last_zone, zone_cols(0)),
    )
    share_cols(FOURTH)
    share_rows(FOURTH)

    all_d = from_cols(FINAL_HUB)
    ones = receive_one(FINAL_HUB, 2 * n_h2)
    sums = jnp.concatenate([ones[0, 0:n_h1], ones[1, 0:n_h1]], axis=0)
    sums_slope = jnp.concatenate([ones[0, n_h1 : 2 * n_h1], ones[1, n_h1 : 2 * n_h1]], axis=0)
    sums = sums - 2.0 * last_b * sums_slope
    two_sum = all_d[0:n_h2] + 2.0 * last_b * all_d[n_h2 : 2 * n_h2]
    got_g = m.got_g
    got_g[r] = adj_b + STEP * (two_sum - sums)
    sems = m.g_out.at[0], m.g_in.at[0]
    loop(n_row - 1, lambda k: put(got_g.at[r], got_g.at[r], *sems, lax.rem(r + k + 1, n_row), c))

    def end_one(rows, lanes, keep, j):
        lane = last_a[j : j + 1]
        theta = grad_one[rows, lanes] + lane * m.z1[rows, lanes]
        cost = grad_cost_one[rows, lanes] - lane * m.b1[rows, lanes]
        return [], [], [(grad_one, theta), (grad_cost_one, cost)]

    def end_two(rows, lanes, keep, j):
        side = m.side_hub[rows, :]
        theta = grad_two[rows, lanes] + side * m.z2[rows, lanes]
        cost = grad_cost_two[rows, lanes] - side * m.b2[rows, lanes]
        return [], [], [(grad_two, theta), (grad_cost_two, cost)]

    sweep_one(end_one, 0, 0)
    sweep_two(end_two, 0, 0)

    grad_depot[...] = adj_depot * grow_depot_0 - STEP * from_cols(FOURTH)
    grad_zone[...] = adj_zone * grow_zone_0 + STEP * from_rows(FOURTH)
    arrived(got_g.at[pl.ds(0, n_row - 1)], m.g_in.at[0])
    for k in range(n_row):
        grad_hub[k * n_h2 : (k + 1) * n_h2, :] = got_g[k]

    arrived(got_g.at[pl.ds(0, n_row - 1)], m.g_out.at[0])
    for t in range(6):
        arrived(m.got_d[t].at[pl.ds(0, n_col - 1)], m.d_out.at[t])
        if t != FINAL_HUB:
            arrived(m.got_z[t].at[pl.ds(0, n_row - 1)], m.z_out.at[t])
        if t in (FIRST, THIRD, FINAL_HUB):

            @pl.when(r != other)
            def _():
                arrived(m.got_h1[t], m.h1_out.at[t])

        if t in (FIRST, THIRD):
            arrived(m.got_h2[t].at[pl.ds(0, n_row)], m.h2_out.at[t])

            @pl.when(r != other)
            def _():
                arrived(m.got_h2[t].at[pl.ds(0, n_row)], m.h2_out.at[t])


def write_kernel(*refs):
    count = (len(refs) - 1) // 2
    sem = refs[-1]
    copies = []
    for src, dst in zip(refs[:count], refs[count:-1]):
        rows = src.shape[0]
        parts = 4 if rows >= 512 else 1
        for n in range(parts):
            piece = pl.ds(n * (rows // parts), rows // parts)
            copies.append(pltpu.make_async_copy(src.at[piece], dst.at[piece], sem.at[len(copies)]))
    for copy in copies:
        copy.start()
    for copy in copies:
        copy.wait()


def on_device(n_row, n_col, *args):
    (theta_one, theta_two, cost_one, cost_two, depot, hub, zone, mask_one, mask_two) = args[:9]
    (supply, demand, capacity, cot_one, cot_two, cot_depot, cot_hub, cot_zone) = args[9:]

    def packed(vector):
        return vector.reshape(vector.shape[0] // LANES, LANES)

    depots, hubs_one = theta_one.shape
    hubs_two, zones = theta_two.shape
    n_d, n_z, n_h = depots // LANES, zones // LANES, hub.shape[0] // LANES
    n_h1, n_h2 = hubs_one // LANES, hubs_two // LANES
    one, two = (depots, hubs_one), (hubs_two, zones)

    def rounded(rows):
        return -(-rows // 8) * 8

    def vec(rows, dtype=F32):
        return pltpu.VMEM((rows, LANES), dtype)

    dma = pltpu.SemaphoreType.DMA
    bf16 = jnp.bfloat16
    hubs = n_h1 + n_h2
    rows_d = [rounded(v) for v in (n_d + hubs, n_d, 2 * n_d, hubs, 2 * hubs, n_d)]
    rows_z = [rounded(v) for v in (n_z + hubs, n_z, 2 * n_z, hubs, 8, n_z)]
    rows_h = [n_h1, 0, 0, n_h1, 2 * n_h1, 0]

    def state():
        return pltpu.VMEM(one, F32)

    def state_two():
        return pltpu.VMEM(two, F32)

    def each(shape_of, rows):
        return [pltpu.VMEM(shape_of(v), F32) if v else None for v in rows]

    scratch = dict(
        th1=pltpu.VMEM(one, bf16),
        th2=pltpu.VMEM(two, bf16),
        co1=pltpu.VMEM(one, bf16),
        co2=pltpu.VMEM(two, bf16),
        ct1=pltpu.VMEM(one, bf16),
        ct2=pltpu.VMEM(two, bf16),
        mask_one=pltpu.SMEM((n_h1, n_d), jnp.int32),
        mask_two=pltpu.SMEM((n_h2, n_z), jnp.int32),
        depot=vec(n_d),
        hub=vec(n_h),
        zone=vec(n_z),
        supply=vec(n_d, jnp.int32),
        demand=vec(n_z, jnp.int32),
        capacity=vec(n_h, jnp.int32),
        cot_depot=vec(n_d),
        cot_hub=vec(n_h),
        cot_zone=vec(n_z),
        side_depot=vec(depots),
        side_last=vec(depots),
        side_hub=vec(hubs_two),
        side_push=vec(hubs_two),
        side_cap=vec(hubs_two),
        lane_zone=pltpu.VMEM((2, n_z, LANES), F32),
        stage_depot=pltpu.VMEM((3, depots, LANES), F32),
        stage_hub=pltpu.VMEM((1, hubs_two, LANES), F32),
        stage_zone=pltpu.VMEM((3, n_z, 8, LANES), F32),
        got_g=pltpu.VMEM((n_row, n_h2, LANES), F32),
        a1=state(),
        b1=state(),
        z1=state(),
        w1=state(),
        a2=state_two(),
        b2=state_two(),
        z2=state_two(),
        w2=state_two(),
        send_d=each(lambda v: (v, LANES), rows_d),
        got_d=each(lambda v: (n_col, v, LANES), rows_d),
        send_z=each(lambda v: (v, LANES), rows_z),
        got_z=each(lambda v: (n_row, v, LANES), rows_z),
        send_h1=each(lambda v: (v, LANES), rows_h),
        got_h1=each(lambda v: (n_row, 2, v, LANES), rows_h),
        send_h2=each(lambda v: (2, v, LANES), rows_h),
        got_h2=each(lambda v: (n_col, v, LANES), rows_h),
        load_sem=dma((4,)),
        two_sem=dma((n_h2, 2)),
        small_sem=dma((11,)),
        g_out=dma((1,)),
        g_in=dma((1,)),
        d_out=dma((6,)),
        d_in=dma((6,)),
        z_out=dma((6,)),
        z_in=dma((6,)),
        h1_out=dma((6,)),
        h1_in=dma((6,)),
        h2_out=dma((6,)),
        h2_in=dma((6,)),
    )
    scratch, tree = jax.tree.flatten(scratch)

    any_spec = pl.BlockSpec(memory_space=pl.ANY)
    vmem = pl.BlockSpec(memory_space=pltpu.VMEM)
    shapes = [one, two, one, two, (n_d, LANES), (n_h, LANES), (n_z, LANES)]
    held = pl.pallas_call(
        functools.partial(main_kernel, n_row, n_col, 17, 7, tree),
        out_shape=[pltpu.VMEM(shape, F32) for shape in shapes],
        in_specs=[any_spec] * 17,
        out_specs=[vmem] * 7,
        scratch_shapes=scratch,
        compiler_params=pltpu.CompilerParams(
            collective_id=0, has_side_effects=True, vmem_limit_bytes=50 * 1024 * 1024
        ),
    )(
        theta_one,
        theta_two,
        cost_one,
        cost_two,
        packed(depot),
        packed(hub),
        packed(zone),
        mask_one.T,
        mask_two,
        packed(supply),
        packed(demand),
        packed(capacity),
        cot_one,
        cot_two,
        packed(cot_depot),
        packed(cot_hub),
        packed(cot_zone),
    )
    outs = pl.pallas_call(
        write_kernel,
        out_shape=[jax.ShapeDtypeStruct(shape, F32) for shape in shapes],
        in_specs=[vmem] * 7,
        out_specs=[any_spec] * 7,
        scratch_shapes=[dma((19,))],
        compiler_params=pltpu.CompilerParams(vmem_limit_bytes=4 * 1024 * 1024),
    )(*[pltpu.with_memory_space_constraint(v, pltpu.VMEM) for v in held])
    return tuple(outs[:4]) + tuple(v.reshape(-1) for v in outs[4:])


def solution(mesh):
    n_row, n_col = mesh.shape["row"], mesh.shape["col"]
    block, by_row, by_col = P("row", "col"), P("row"), P("col")
    return jax.shard_map(
        functools.partial(on_device, n_row, n_col),
        mesh=mesh,
        in_specs=(
            (block,) * 4 + (by_row, P(), by_col, block, block, by_row, by_col, P(), block, block)
            + (by_row, P(), by_col)
        ),
        out_specs=(block,) * 4 + (by_row, P(), by_col),
        check_vma=False,
    )
```

time: 392 us -> 42 us (0.11)
  blocking collectives: 340 us -> 0 us
  other arithmetic: 46.9 us -> 0 us
  Pallas kernels: 0 us -> 41.2 us
    psum x8 -> x0, blocking collectives: 210 us -> none  [the longest x4 152 us: dual_sums(): depot_sum, hub_two_sum = lax.psum((depot_part, hub_two_part), 'col')]
    all_gather x6 -> x0, blocking collectives: 131 us -> none  [the longest x3 73.2 us: dual_sums(): lax.all_gather(hub_one_sum, 'col', axis=0, tiled=True)]
    pallas_call x0 -> x2, Pallas kernels: none -> 41.2 us  [the longest x1 37.1 us: on_device(): pl.pallas_call(functools.partial(main_kernel, n_row, n_col, 17, 7, tree),...]
    reduce_sum x8 -> x0, other arithmetic: 33.8 us -> none  [the longest x2 14 us: on_device(): jnp.sum(total_two, axis=0)]
    sub x3 -> x0, other arithmetic: 8.74 us -> none  [the longest x1 6.23 us: on_device(): grad_second = grad_second - STEP_PRIMAL * total_two]
where the time goes in v2:
time: 42 us; the launch traced here: 41.8 us
  Pallas kernels  41.2 us (98%)
  between operations  0.65 us (2%)
    pallas_call x1, Pallas kernels, on_device(): pl.pallas_call(functools.partial(main_kernel, n_row, n_col, 17, 7, tree),...  37.1 us
    pallas_call x1, Pallas kernels, on_device(): pl.pallas_call(write_kernel, out_shape=[jax.ShapeDtypeStruct(shape, F32)...  4.1 us

profile of v2, /device:TPU:1, one launch (start us, length us, event | category | flops | bytes accessed | tf_op | source)
XLA Modules:
  0.0 41.8 jit_solution(14436372749787098919)
XLA Ops:
  0.6 37.1 %shard_map.216 = (f32[1024,256]{1,0:T(8,128)S(1)}, f32[512,2048]{1,0:T(8,128)S(1)}, f32[1024,256]{1,0:T(8,128)S(1)}, f32[512,2048]{1,0:T(8,128)S(1)}, f32[8,128]...) custom-call(bf16[1024,256]{1,0:T(8,128)(2,1)} %refs_0_.1, bf16[512,2048]{1,0:T(8,128)(2,1)} %refs_1_.1, ...), custom_call_target="tpu_custom_call" | custom-call | tf_op jit(solution)/shard_map/pallas_call | solution.py:738
  37.7 4.1 %shard_map.217 = (f32[1024,256]{1,0:T(8,128)}, f32[512,2048]{1,0:T(8,128)}, f32[1024,256]{1,0:T(8,128)}, f32[512,2048]{1,0:T(8,128)}, f32[8,128]{1,0:T(8,128)}, /*index=5*/f32[32,128]{1,0:T(8,128)}, f32[16,128]{1,0:T(8,128)}) custom-call(f32[1024,256]{1,0:T(8,128)S(1)} %get-tuple-element.21.refs_0_, f32[512,2048]{1,0:T(8,128)S(1)} %get-tuple-element.22.refs_1_, ...), custom_call_target="tpu_custom_call" | custom-call | tf_op jit(solution)/shard_map/pallas_call | solution.py:766

commit v3 on v2

--- a/solution.py
+++ b/solution.py
@@ -421,8 +421,6 @@
     hub_b = hub_b + two_here * (HUB_RATE / DEP)
 
     set_side(m.side_depot, 0.25 * depot_0)
-    set_side(m.side_hub, 0.25 * hub_b)
-    m.lane_zone[0] = 0.25 * zone_0
     lane_one_next = 0.25 * hub_a
 
     def second_one(rows, lanes, keep, j):
@@ -434,10 +432,12 @@
         return [], [keep * t_new], [(m.a2, t_new)]
 
     sweep_one(second_one, 1, 0)
+    fill(m.send_d[1], depot_rows(0) + past_depot)
+    share_cols(SECOND)
+    set_side(m.side_hub, 0.25 * hub_b)
+    m.lane_zone[0] = 0.25 * zone_0
     sweep_two(second_two, 0, 1)
-    fill(m.send_d[1], depot_rows(0) + past_depot)
     fill(m.send_z[1], zone_cols(0) + past_zone)
-    share_cols(SECOND)
     share_rows(SECOND)
 
     for copy in late:
@@ -457,13 +457,13 @@
 
     (alpha_a,) = sweep_one(linear_one, 2, 1)
     alpha_depot, beta_depot = depot_rows(0), depot_rows(1)
+    fill(m.send_d[2], alpha_depot, beta_depot)
+    share_cols(LINEAR)
     sweep_two(linear_two, 1, 2)
     alpha_zone, beta_zone = zone_cols(0), zone_cols(1)
+    fill(m.send_z[2], alpha_zone, beta_zone)
+    share_rows(LINEAR)
     alpha_b = hub_rows(0)
-    fill(m.send_d[2], alpha_depot, beta_depot)
-    fill(m.send_z[2], alpha_zone, beta_zone)
-    share_cols(LINEAR)
-    share_rows(LINEAR)
 
     grow_depot_1 = jnp.exp(STEP * (from_cols(SECOND) * (1.0 / HUB) - supply_level))
     grow_zone_1 = jnp.exp(STEP * (demand_level - from_rows(SECOND) * (1.0 / HUB)))
@@ -518,25 +518,6 @@
         part = weight * slope
         return total - part + last * mixed, 0.5 * part - total - last * slope
 
-    def state_one(rows, lanes, keep, j):
-        twice = m.side_depot[rows, :]
-        total = m.w1[rows, lanes] + twice * m.a1[rows, lanes]
-        weight = 0.5 * twice + push_a[j : j + 1]
-        theta, cost = state(
-            total, weight, m.side_last[rows, :], m.b1[rows, lanes], m.z1[rows, lanes]
-        )
-        return [], [], [(grad_one, theta), (grad_cost_one, cost)]
-
-    def state_two(rows, lanes, keep, j):
-        twice = zone_lane(0, j)
-        total = m.w2[rows, lanes] + twice * m.a2[rows, lanes]
-        weight = 0.5 * twice + m.side_push[rows, :]
-        theta, cost = state(total, weight, zone_lane(1, j), m.b2[rows, lanes], m.z2[rows, lanes])
-        return [], [], [(grad_two, theta), (grad_cost_two, cost)]
-
-    sweep_one(state_one, 0, 0)
-    sweep_two(state_two, 0, 0)
-
     all_d = from_cols(THIRD)
     all_z = from_rows(THIRD)
     one_here, two_here = receive_hubs(THIRD, all_d, all_z, 0, 0)
@@ -545,29 +526,29 @@
     last_a = adj_a * (HUB_RATE / DEP)
     last_b = adj_b * (-HUB_RATE / DEP)
 
-    set_side(m.side_hub, last_b)
-
     def fourth_one(rows, lanes, keep, j):
         return [m.b1[rows, lanes] * last_a[j : j + 1]], [], []
 
     def fourth_two(rows, lanes, keep, j):
         return [], [m.b2[rows, lanes] * m.side_hub[rows, :]], []
 
-    sweep_one(fourth_one, 1, 0)
-    sweep_two(fourth_two, 0, 1)
-
     def last_sum(alpha, beta, push, slope, pushed, last, value):
         return alpha + 2.0 * push * beta + (2.0 * last - push) * slope - pushed + 2.0 * value
 
+    sweep_one(fourth_one, 1, 0)
+    depot_value = depot_rows(0)
     fill(
         m.send_d[5],
-        last_sum(alpha_depot, beta_depot, push_depot, slope_depot, pushed_depot, last_depot, depot_rows(0)),
-    )
+        last_sum(alpha_depot, beta_depot, push_depot, slope_depot, pushed_depot, last_depot, depot_value),
+    )
+    share_cols(FOURTH)
+    set_side(m.side_hub, last_b)
+    sweep_two(fourth_two, 0, 1)
+    zone_value = zone_cols(0)
     fill(
         m.send_z[5],
-        last_sum(alpha_zone, beta_zone, push_zone, slope_zone, pushed_zone, last_zone, zone_cols(0)),
-    )
-    share_cols(FOURTH)
+        last_sum(alpha_zone, beta_zone, push_zone, slope_zone, pushed_zone, last_zone, zone_value),
+    )
     share_rows(FOURTH)
 
     all_d = from_cols(FINAL_HUB)
@@ -582,15 +563,19 @@
     loop(n_row - 1, lambda k: put(got_g.at[r], got_g.at[r], *sems, lax.rem(r + k + 1, n_row), c))
 
     def end_one(rows, lanes, keep, j):
-        lane = last_a[j : j + 1]
-        theta = grad_one[rows, lanes] + lane * m.z1[rows, lanes]
-        cost = grad_cost_one[rows, lanes] - lane * m.b1[rows, lanes]
+        twice = m.side_depot[rows, :]
+        total = m.w1[rows, lanes] + twice * m.a1[rows, lanes]
+        weight = 0.5 * twice + push_a[j : j + 1]
+        last = m.side_last[rows, :] + last_a[j : j + 1]
+        theta, cost = state(total, weight, last, m.b1[rows, lanes], m.z1[rows, lanes])
         return [], [], [(grad_one, theta), (grad_cost_one, cost)]
 
     def end_two(rows, lanes, keep, j):
-        side = m.side_hub[rows, :]
-        theta = grad_two[rows, lanes] + side * m.z2[rows, lanes]
-        cost = grad_cost_two[rows, lanes] - side * m.b2[rows, lanes]
+        twice = zone_lane(0, j)
+        total = m.w2[rows, lanes] + twice * m.a2[rows, lanes]
+        weight = 0.5 * twice + m.side_push[rows, :]
+        last = zone_lane(1, j) + m.side_hub[rows, :]
+        theta, cost = state(total, weight, last, m.b2[rows, lanes], m.z2[rows, lanes])
         return [], [], [(grad_two, theta), (grad_cost_two, cost)]
 
     sweep_one(end_one, 0, 0)

time: 42 us -> 40.6 us (0.967)
  Pallas kernels: 41.2 us -> 39.8 us
    pallas_call x1, Pallas kernels: 37.1 us -> 35.7 us  [on_device(): pl.pallas_call(functools.partial(main_kernel, n_row, n_col, 17, 7, tree),...]
where the time goes in v3:
time: 40.6 us; the launch traced here: 40.5 us
  Pallas kernels  39.8 us (98%)
  between operations  0.65 us (2%)
    pallas_call x1, Pallas kernels, on_device(): pl.pallas_call(functools.partial(main_kernel, n_row, n_col, 17, 7, tree),...  35.7 us
    pallas_call x1, Pallas kernels, on_device(): pl.pallas_call(write_kernel, out_shape=[jax.ShapeDtypeStruct(shape, F32)...  4.1 us

profile of v3, /device:TPU:1, one launch (start us, length us, event | category | flops | bytes accessed | tf_op | source)
XLA Modules:
  0.0 40.5 jit_solution(15230435018122987525)
XLA Ops:
  0.6 35.7 %shard_map.216 = (f32[1024,256]{1,0:T(8,128)S(1)}, f32[512,2048]{1,0:T(8,128)S(1)}, f32[1024,256]{1,0:T(8,128)S(1)}, f32[512,2048]{1,0:T(8,128)S(1)}, f32[8,128]...) custom-call(bf16[1024,256]{1,0:T(8,128)(2,1)} %refs_0_.1, bf16[512,2048]{1,0:T(8,128)(2,1)} %refs_1_.1, ...), custom_call_target="tpu_custom_call" | custom-call | tf_op jit(solution)/shard_map/pallas_call | solution.py:723
  36.4 4.1 %shard_map.217 = (f32[1024,256]{1,0:T(8,128)}, f32[512,2048]{1,0:T(8,128)}, f32[1024,256]{1,0:T(8,128)}, f32[512,2048]{1,0:T(8,128)}, f32[8,128]{1,0:T(8,128)}, /*index=5*/f32[32,128]{1,0:T(8,128)}, f32[16,128]{1,0:T(8,128)}) custom-call(f32[1024,256]{1,0:T(8,128)S(1)} %get-tuple-element.21.refs_0_, f32[512,2048]{1,0:T(8,128)S(1)} %get-tuple-element.22.refs_1_, ...), custom_call_target="tpu_custom_call" | custom-call | tf_op jit(solution)/shard_map/pallas_call | solution.py:751
